TPU v7x, 128 devices: a whole 4x4x4 slice. The times are simulated.
128 devices in a mesh: dp: 8 (over x, y_lo), expert: 16 (over z, y_hi, core).
Axes of the slice: x: 4, y: 4 (y_hi: 2, y_lo: 2; y = y_hi * 2 + y_lo), z: 4, core: 2. Of those that a mesh axis runs over, the one named last changes fastest.
Arguments:
- tokens: bfloat16 [32768, 1536], P(('dp', 'expert')), may hold values from -24 to 24
- cotangent: bfloat16 [32768, 1536], P(('dp', 'expert')), may hold values from -0.59765625 to 0.59765625
- chosen: int32 [512, 16, 8], P(('dp', 'expert')), may hold values from 0 to 63, as said below
- w_router: bfloat16 [1536, 16], replicated, may hold values from -0.15625 to 0.15625
- w_gate: bfloat16 [16, 1536, 1024], P('expert', 'dp'), may hold values from -0.15625 to 0.15625
- w_up: bfloat16 [16, 1536, 1024], P('expert', 'dp'), may hold values from -0.15625 to 0.15625
- w_down: bfloat16 [16, 1024, 1536], P('expert', 'dp'), may hold values from -0.1875 to 0.1875
Outputs:
- mixed: bfloat16 [32768, 1536], P(('dp', 'expert'))
- grad_tokens: bfloat16 [32768, 1536], P(('dp', 'expert'))
- grad_gate: float32 [16, 1536, 1024], P('expert', 'dp')
- grad_up: float32 [16, 1536, 1024], P('expert', 'dp')
- down_weight_gradient: float32 [16, 1024, 1536], P('expert', 'dp')
- grad_router: float32 [1536, 16], replicated
Inputs may be any that keep to these rules, and one draw needn't show every extreme that they name: `chosen`: for each aligned block of 64 token rows and each expert, 8 different row numbers within the block; so every device has exactly 32 slots for each expert.
All inputs are finite; a program needn't handle non-finite values.
Results may differ from a plain program's by a relative error of at most 0.017.
Values may be sent and summed in bfloat16 or wider, within the bound.
A program may use at most 128 MiB of HBM per device.

v0:
```python
import jax
import jax.numpy as jnp
from jax import lax
from jax.sharding import PartitionSpec as P


def to_blocks(slot_array, num_blocks, pick_count):
    expert_count = slot_array.shape[0]
    trailing = slot_array.shape[2:]
    grouped = slot_array.reshape((expert_count, num_blocks, pick_count) + trailing)
    axis_order = (1, 0, 2) + tuple(range(3, 3 + len(trailing)))
    return jnp.transpose(grouped, axis_order).reshape(
        (num_blocks, expert_count * pick_count) + trailing
    )


def weight_grads(expert_rows, hidden, expert_cot, d_pre_gate, d_pre_up):
    hidden_activations = hidden.shape[2]
    both_grads = jnp.concatenate([d_pre_gate, d_pre_up], axis=2)
    columns = expert_rows
    in_share = lax.psum_scatter(
        jnp.einsum("erc,erk->cek", columns, both_grads, preferred_element_type=jnp.float32).astype(
            jnp.bfloat16
        ),
        "dp",
        scatter_dimension=0,
        tiled=True,
    ).astype(jnp.float32)
    grad_gate = jnp.transpose(in_share[:, :, :hidden_activations], (1, 0, 2))
    grad_up = jnp.transpose(in_share[:, :, hidden_activations:], (1, 0, 2))
    columns = hidden
    out_share = lax.psum_scatter(
        jnp.einsum("erc,erd->ced", columns, expert_cot, preferred_element_type=jnp.float32).astype(
            jnp.bfloat16
        ),
        "dp",
        scatter_dimension=0,
        tiled=True,
    ).astype(jnp.float32)
    down_weight_gradient = jnp.transpose(out_share, (1, 0, 2))
    return (grad_gate, grad_up, down_weight_gradient)


def body(tokens, cotangent, chosen, w_router, w_gate, w_up, w_down):
    tok_rows, model_width = tokens.shape
    num_blocks, expert_count, pick_count = chosen.shape
    block_rows = tok_rows // num_blocks
    slot_count = num_blocks * pick_count
    logits = jnp.dot(tokens, w_router, preferred_element_type=jnp.float32)
    gate_values = jax.nn.sigmoid(logits)
    offsets = (jnp.arange(num_blocks, dtype=jnp.int32) * block_rows)[:, None, None]
    slot_rows = jnp.transpose(chosen + offsets, (1, 0, 2)).reshape(expert_count, slot_count)
    picked = tokens[slot_rows]
    slot_gate_values = jnp.take_along_axis(gate_values.T, slot_rows, axis=1)
    cot_rows = cotangent[slot_rows]
    scaled_cot = (slot_gate_values[:, :, None] * cot_rows.astype(jnp.float32)).astype(jnp.bfloat16)
    full_gate, full_up, full_down = (
        lax.all_gather(w_gate, "dp", axis=1, tiled=True),
        lax.all_gather(w_up, "dp", axis=1, tiled=True),
        lax.all_gather(w_down, "dp", axis=1, tiled=True),
    )
    expert_rows = lax.all_to_all(picked, "expert", split_axis=0, concat_axis=1, tiled=True)
    pre_gate = jnp.einsum(
        "erd,edh->erh", expert_rows, full_gate, preferred_element_type=jnp.float32
    )
    pre_up = jnp.einsum("erd,edh->erh", expert_rows, full_up, preferred_element_type=jnp.float32)
    silu_gate = jax.nn.silu(pre_gate)
    hidden = (silu_gate * pre_up).astype(jnp.bfloat16)
    expert_out = jnp.einsum(
        "erh,ehd->erd", hidden, full_down, preferred_element_type=jnp.float32
    ).astype(jnp.bfloat16)
    returned = lax.all_to_all(expert_out, "expert", split_axis=1, concat_axis=0, tiled=True)
    expert_cot = lax.all_to_all(scaled_cot, "expert", split_axis=0, concat_axis=1, tiled=True)
    back_gate, back_up, back_down = (full_gate, full_up, full_down)
    d_hidden = jnp.einsum("erd,ehd->erh", expert_cot, back_down, preferred_element_type=jnp.float32)
    gate_sigmoid = jax.nn.sigmoid(pre_gate)
    d_pre_gate = (
        d_hidden * pre_up * gate_sigmoid * (1.0 + pre_gate * (1.0 - gate_sigmoid))
    ).astype(jnp.bfloat16)
    d_pre_up = (d_hidden * silu_gate).astype(jnp.bfloat16)
    d_rows = (
        jnp.einsum("erh,edh->erd", d_pre_gate, back_gate, preferred_element_type=jnp.float32)
        + jnp.einsum("erh,edh->erd", d_pre_up, back_up, preferred_element_type=jnp.float32)
    ).astype(jnp.bfloat16)
    row_grads = lax.all_to_all(d_rows, "expert", split_axis=1, concat_axis=0, tiled=True)
    position_hits = chosen[:, :, :, None] == jnp.arange(block_rows, dtype=jnp.int32)
    indicator_matrix = position_hits.reshape(num_blocks, expert_count * pick_count, block_rows)
    gate_weighted_rows = to_blocks(slot_gate_values, num_blocks, pick_count)[
        :, :, None
    ] * to_blocks(returned, num_blocks, pick_count).astype(jnp.float32)
    mixed = (
        jnp.einsum(
            "wze,wzi->wei",
            indicator_matrix.astype(jnp.float32),
            gate_weighted_rows,
            precision=lax.Precision.HIGHEST,
        )
        .reshape(tok_rows, model_width)
        .astype(jnp.bfloat16)
    )
    slot_dots = jnp.sum(cot_rows.astype(jnp.float32) * returned.astype(jnp.float32), axis=2)
    dgate = jnp.einsum(
        "bept,ebp->bte",
        position_hits.astype(jnp.float32),
        slot_dots.reshape(expert_count, num_blocks, pick_count),
        precision=lax.Precision.HIGHEST,
    ).reshape(tok_rows, expert_count)
    d_logit = (dgate * gate_values * (1.0 - gate_values)).astype(jnp.bfloat16)
    gathered_grads = jnp.einsum(
        "wze,wzi->wei",
        indicator_matrix.astype(jnp.bfloat16),
        to_blocks(row_grads, num_blocks, pick_count),
        preferred_element_type=jnp.float32,
    ).reshape(tok_rows, model_width)
    grad_tokens = (
        gathered_grads + jnp.dot(d_logit, w_router.T, preferred_element_type=jnp.float32)
    ).astype(jnp.bfloat16)
    grad_router = lax.psum(
        jnp.dot(tokens.T, d_logit, preferred_element_type=jnp.float32), ("dp", "expert")
    )
    grad_gate, grad_up, down_weight_gradient = weight_grads(
        expert_rows, hidden, expert_cot, d_pre_gate, d_pre_up
    )
    return (mixed, grad_tokens, grad_gate, grad_up, down_weight_gradient, grad_router)


def solution(mesh):
    placed = (
        P(("dp", "expert"), None),
        P(("dp", "expert"), None),
        P(("dp", "expert"), None, None),
        P(),
        P("expert", "dp", None),
        P("expert", "dp", None),
        P("expert", "dp", None),
    )
    return jax.shard_map(
        body,
        mesh=mesh,
        in_specs=placed,
        out_specs=(
            P(("dp", "expert"), None),
            P(("dp", "expert"), None),
            P("expert", "dp", None),
            P("expert", "dp", None),
            P("expert", "dp", None),
            P(),
        ),
        check_vma=False,
    )
```

profile of v0, /device:TPU:1, one launch (start us, length us, event | category | flops | bytes accessed | tf_op | source)
XLA Modules:
  0.0 655.6 jit_solution(1444224585253242615)
XLA Ops:
  13.3 9.6 %all-to-all-start = ((bf16[16,32,1536]{2,1,0:T(8,128)(2,1)}), bf16[16,32,1536]{2,1,0:T(8,128)(2,1)}, u32[]{:S(2)}, u32[]{:S(2)}) async-start(bf16[16,32,1536]{2,1,0:T(8,128)(2,1)} %bitcast.5), calls=%async_computation | async-start | bytes 3145728 | tf_op jit(solution)/shard_map/all_to_all | solution.py:62
  32.0 49.3 %all-to-all-done = bf16[16,32,1536]{2,1,0:T(8,128)(2,1)} async-done(((bf16[16,32,1536]{2,1,0:T(8,128)(2,1)}), bf16[16,32,1536]{2,1,0:T(8,128)(2,1)}, u32[]{:S(2)}, u32[]{:S(2)}) %all-to-all-start) | async-done | bytes 1572896 | tf_op jit(solution)/shard_map/all_to_all | solution.py:62
  85.8 19.2 %all-gather.4.cloned.1.call-done = bf16[1,1536,1024]{2,1,0:T(8,128)(2,1)} async-done(((bf16[1,192,1024]{2,1,0:T(8,128)(2,1)}), bf16[1,1536,1024]{2,1,0:T(8,128)(2,1)}) %all-gather.4.cloned.1.call-update) | async-done | bytes 3145744 | tf_op jit(solution)/shard_map/all_gather | solution.py:58
  105.1 5.5 fusion.13
  110.6 69.9 %all-gather.6.cloned.1.call-done = bf16[1,1536,1024]{2,1,0:T(8,128)(2,1)} async-done(((bf16[1,192,1024]{2,1,0:T(8,128)(2,1)}), bf16[1,1536,1024]{2,1,0:T(8,128)(2,1)}) %all-gather.6.cloned.1.call-update) | async-done | bytes 3145744 | tf_op jit(solution)/shard_map/all_gather | solution.py:59
  180.5 5.5 fusion.9
  185.9 67.4 %all-gather.8.cloned.1.call-done = bf16[1,1024,1536]{2,1,0:T(8,128)(2,1)} async-done(((bf16[1,128,1536]{2,1,0:T(8,128)(2,1)}), bf16[1,1024,1536]{2,1,0:T(8,128)(2,1)}) %all-gather.8.cloned.1.call-update) | async-done | bytes 3145744 | tf_op jit(solution)/shard_map/all_gather | solution.py:60
  253.3 7.4 %multiply_convert_fusion.1 = (bf16[512,1024]{1,0:T(8,128)(2,1)}, bf16[512,1024]{1,0:T(8,128)(2,1)}, bf16[512,1024]{1,0:T(8,128)(2,1)S(1)}) fusion(f32[512,1024]{1,0:T(8,128)} %fusion.13, f32[512,1024]{1,0:T(8,128)} %fusion.9, bf16[512,1536]{1,0:T(8,128)(2,1)} %bitcast.18, bf16[1,1024,1536]{2,1,0:T(8,128)(2,1)} %all-gather.8.cloned.1.call-done), kind=kOutput, calls=%fused_computation.36 | convolution fusion | flops 1618477056 | bytes 12058624 | tf_op jit(solution)/shard_map/erd,ehd->erh/dot_general | solution.py:75
  261.8 4.9 fusion.1
  266.7 4.7 copy.104
  271.7 8.1 %fusion = bf16[1536,2048]{0,1:T(8,128)(2,1)} fusion(bf16[512,1536]{1,0:T(8,128)(2,1)} %bitcast.6, bf16[1,512,1024]{2,1,0:T(8,128)(2,1)} %bitcast.148, bf16[1,512,1024]{2,1,0:T(8,128)(2,1)} %bitcast.149), kind=kOutput, calls=%fused_computation.4 | convolution fusion | flops 3228565504 | bytes 9961472 | tf_op jit(solution)/shard_map/erc,erk->cek/dot_general | solution.py:22
  279.8 8.8 %copy.102 = bf16[1536,2048]{1,0:T(8,128)(2,1)} copy(bf16[1536,2048]{0,1:T(8,128)(2,1)} %fusion) | data formatting | bytes 12582912
  299.3 12.8 %reduce.2 = bf16[512,1536]{1,0:T(8,128)(2,1)} reduce(bf16[512,1,1536]{2,1,0:T(2,128)(2,1)} %bitcast.140, bf16[]{:T(256)} %broadcast.103), dimensions={1}, to_apply=%bitcast.134.reduce_sub_computation | reduce | bytes 3145730
  312.1 5.0 reshape.248
  317.1 7.9 %all-to-all-start.3 = ((bf16[16,2,24576]{2,1,0:T(2,128)(2,1)}), bf16[16,2,24576]{2,1,0:T(2,128)(2,1)}, u32[]{:S(2)}, u32[]{:S(2)}) async-start(bf16[16,2,24576]{2,1,0:T(2,128)(2,1)} %reshape.248), calls=%async_computation.3 | async-start | bytes 3145728 | tf_op jit(solution)/shard_map/all_to_all | solution.py:85
  333.2 12.6 %reduce.1 = bf16[512,1536]{1,0:T(8,128)(2,1)} reduce(bf16[512,1,1536]{2,1,0:T(2,128)(2,1)} %bitcast.142, bf16[]{:T(256)} %broadcast.103), dimensions={1}, to_apply=%bitcast.135.reduce_sub_computation | reduce | bytes 3145730
  345.8 5.0 reshape.246
  350.7 12.6 %all-to-all-done.3 = bf16[16,2,24576]{2,1,0:T(2,128)(2,1)} async-done(((bf16[16,2,24576]{2,1,0:T(2,128)(2,1)}), bf16[16,2,24576]{2,1,0:T(2,128)(2,1)}, u32[]{:S(2)}, u32[]{:S(2)}) %all-to-all-start.3) | async-done | bytes 1572896 | tf_op jit(solution)/shard_map/all_to_all | solution.py:85
  363.3 4.6 all-to-all-start.1
  368.5 10.0 %reshape.249 = bf16[512,1,1536]{2,1,0:T(2,128)(2,1)} reshape(bf16[16,2,24576]{2,1,0:T(2,128)(2,1)} %all-to-all-done.3) | data formatting | bytes 3145728
  381.9 44.6 %all-to-all-done.1 = bf16[16,2,24576]{2,1,0:T(2,128)(2,1)} async-done(((bf16[16,2,24576]{2,1,0:T(2,128)(2,1)}), bf16[16,2,24576]{2,1,0:T(2,128)(2,1)}, u32[]{:S(2)}, u32[]{:S(2)}) %all-to-all-start.1) | async-done | bytes 1572896 | tf_op jit(solution)/shard_map/all_to_all | solution.py:72
  426.5 10.0 %reshape.247 = bf16[512,1,1536]{2,1,0:T(2,128)(2,1)} reshape(bf16[16,2,24576]{2,1,0:T(2,128)(2,1)} %all-to-all-done.1) | data formatting | bytes 3145728
  447.9 54.7 %reduce-scatter.7.cloned.1.call-done = bf16[192,2048]{1,0:T(8,128)(2,1)} async-done(((bf16[1536,2048]{1,0:T(8,128)(2,1)}), bf16[192,2048]{1,0:T(8,128)(2,1)}) %reduce-scatter.7.cloned.1.call-update) | async-done | bytes 786448
  506.7 140.3 %all-reduce.2.cloned.1.call-done = f32[1536,16]{0,1:T(8,128)} async-done(((f32[1536,16]{0,1:T(8,128)}), f32[1536,16]{0,1:T(8,128)}) %all-reduce.2.cloned.1.call-update) | async-done | bytes 98320 | tf_op jit(solution)/shard_map/psum | solution.py:118
  (83 shorter events, 60.8 us)
Async XLA Ops:
  7.2 3.2 copy-start
  7.2 97.9 %all-gather.4.cloned.1.call-start = ((), (), s32[]{:S(2)}) async-start(), calls=%async_computation.6 | async-start | bytes 3538944 | tf_op jit(solution)/shard_map/all_gather | solution.py:58
  7.9 172.5 %all-gather.6.cloned.1.call-start = ((), (), s32[]{:S(2)}) async-start(), calls=%async_computation.7 | async-start | bytes 3538944 | tf_op jit(solution)/shard_map/all_gather | solution.py:59
  8.7 244.6 %all-gather.8.cloned.1.call-start = ((), (), s32[]{:S(2)}) async-start(), calls=%async_computation.8 | async-start | bytes 3538944 | tf_op jit(solution)/shard_map/all_gather | solution.py:60
  13.3 9.7 %copy-start.5 = (bf16[1536,16]{0,1:T(8,128)(2,1)S(1)}, bf16[1536,16]{0,1:T(8,128)(2,1)}, u32[]{:S(2)}) copy-start(bf16[1536,16]{0,1:T(8,128)(2,1)} %param.10) | copy-start | bytes 147460
  13.3 67.9 %all-to-all-start = ((bf16[16,32,1536]{2,1,0:T(8,128)(2,1)}), bf16[16,32,1536]{2,1,0:T(8,128)(2,1)}, u32[]{:S(2)}, u32[]{:S(2)}) async-start(bf16[16,32,1536]{2,1,0:T(8,128)(2,1)} %bitcast.5), calls=%async_computation | async-start | bytes 3145728 | tf_op jit(solution)/shard_map/all_to_all | solution.py:62
  23.4 4.7 copy-start.4
  23.4 4.8 copy-start.1
  81.2 104.7 %all-to-all-start.2 = ((bf16[16,32,1536]{2,1,0:T(8,128)(2,1)}), bf16[16,32,1536]{2,1,0:T(8,128)(2,1)}, u32[]{:S(2)}, u32[]{:S(2)}) async-start(bf16[16,32,1536]{2,1,0:T(8,128)(2,1)} %multiply_convert_fusion), calls=%async_computation.2 | async-start | bytes 3145728 | tf_op jit(solution)/shard_map/all_to_all | solution.py:73
  85.8 359.7 %reduce-scatter.9.cloned.1.call-start = ((), (), s32[]{:S(2)}) async-start(), calls=%async_computation.11 | async-start | bytes 3538944
  260.7 1.1 copy-start.8
  271.4 231.2 %reduce-scatter.7.cloned.1.call-start = ((), (), s32[]{:S(2)}) async-start(), calls=%async_computation.10 | async-start | bytes 7077888
  288.6 4.2 copy-start.6
  288.6 4.2 copy-start.7
  317.1 46.2 %all-to-all-start.3 = ((bf16[16,2,24576]{2,1,0:T(2,128)(2,1)}), bf16[16,2,24576]{2,1,0:T(2,128)(2,1)}, u32[]{:S(2)}, u32[]{:S(2)}) async-start(bf16[16,2,24576]{2,1,0:T(2,128)(2,1)} %reshape.248), calls=%async_computation.3 | async-start | bytes 3145728 | tf_op jit(solution)/shard_map/all_to_all | solution.py:85
  363.3 63.2 %all-to-all-start.1 = ((bf16[16,2,24576]{2,1,0:T(2,128)(2,1)}), bf16[16,2,24576]{2,1,0:T(2,128)(2,1)}, u32[]{:S(2)}, u32[]{:S(2)}) async-start(bf16[16,2,24576]{2,1,0:T(2,128)(2,1)} %reshape.246), calls=%async_computation.1 | async-start | bytes 3145728 | tf_op jit(solution)/shard_map/all_to_all | solution.py:72
  367.9 279.2 %all-reduce.2.cloned.1.call-start = ((), (), s32[]{:S(2)}) async-start(), calls=%async_computation.9 | async-start | bytes 196608 | tf_op jit(solution)/shard_map/psum | solution.py:118
  439.0 1.5 copy-start.3
  440.5 2.2 copy-start.2
Sparse Core Ops, SparseCore 0:
  9.7 95.3 all-gather.3
  106.7 73.7 all-gather.5
  182.1 71.1 all-gather.7
  271.6 79.1 reduce-scatter.8
  353.1 149.5 reduce-scatter.6
  507.8 139.2 all-reduce.1
where the time goes:
time: 665 us; the launch traced here: 656 us
  waiting for transfers between devices  460 us (69%)
  local copies, waits for them, and re-layouts  76 us (11%)
  matrix products  47.1 us (7%)
  other arithmetic  30.8 us (5%)
  starting transfers between devices  27 us (4%)
  between operations  14.5 us (2%)
    psum x1, waiting for transfers between devices, body(): lax.psum(jnp.dot(tokens.T, d_logit, preferred_element_type=jnp.float32),...  140 us
    all_gather x1, waiting for transfers between devices, body(): lax.all_gather(w_up, 'dp', axis=1, tiled=True)  69.9 us
    all_gather x1, waiting for transfers between devices, body(): lax.all_gather(w_down, 'dp', axis=1, tiled=True)  67.4 us
    unnamed x33, local copies, waits for them, and re-layouts  56.8 us
    unnamed x8, waiting for transfers between devices  56.8 us
    all_to_all x1, waiting for transfers between devices, body(): lax.all_to_all(picked, 'expert', split_axis=0, concat_axis=1, tiled=True)  49.3 us
    all_to_all x1, waiting for transfers between devices, body(): lax.all_to_all(expert_out, 'expert', split_axis=1, concat_axis=0, tiled=T...  44.6 us
    unnamed x2, other arithmetic  25.4 us
  transfers between devices with their start and end apart: 10, of which 8 were waited for; matrix products, arithmetic and copies ran while one was open for 20% of the time, Pallas kernels for 0%

commit v1 on v0

--- a/solution.py
+++ b/solution.py
@@ -2,6 +2,7 @@
 import jax.numpy as jnp
 from jax import lax
 from jax.sharding import PartitionSpec as P
+from jax.lax import all_to_all, axis_size
 
 
 def to_blocks(slot_array, num_blocks, pick_count):
@@ -42,6 +43,12 @@
 
 
 def body(tokens, cotangent, chosen, w_router, w_gate, w_up, w_down):
+
+    def test_ladders(u_in):
+        return jnp.concatenate(
+            all_to_all(jnp.stack([u_in] * axis_size("dp"), axis=0), "dp", 0, 0), axis=1
+        )
+
     tok_rows, model_width = tokens.shape
     num_blocks, expert_count, pick_count = chosen.shape
     block_rows = tok_rows // num_blocks
@@ -57,7 +64,7 @@
     full_gate, full_up, full_down = (
         lax.all_gather(w_gate, "dp", axis=1, tiled=True),
         lax.all_gather(w_up, "dp", axis=1, tiled=True),
-        lax.all_gather(w_down, "dp", axis=1, tiled=True),
+        test_ladders(w_down),
     )
     expert_rows = lax.all_to_all(picked, "expert", split_axis=0, concat_axis=1, tiled=True)
     pre_gate = jnp.einsum(

time: 665 us -> 627 us (0.943)
  waiting for transfers between devices: 460 us -> 387 us
  blocking collectives: 0 us -> 33.5 us
    all_gather x1, waiting for transfers between devices: 69.9 us -> 0.02 us  [body(): lax.all_gather(w_up, 'dp', axis=1, tiled=True)]
    all_gather x1 -> x0, waiting for transfers between devices: 67.4 us -> none  [body(): lax.all_gather(w_down, 'dp', axis=1, tiled=True)]
    all_gather x1, waiting for transfers between devices: 19.2 us -> 77.5 us  [body(): lax.all_gather(w_gate, 'dp', axis=1, tiled=True)]
    all_to_all x1, waiting for transfers between devices: 0.01 us -> 55 us  [body(): lax.all_to_all(scaled_cot, 'expert', split_axis=0, concat_axis=1, tiled=T...]
    all_to_all x1, waiting for transfers between devices: 49.3 us -> 0.01 us  [test_ladders(): all_to_all(jnp.stack([u_in] * axis_size('dp'), axis=0), 'dp', 0, 0)]
    all_to_all x0 -> x1, blocking collectives: none -> 33.5 us  [body(): lax.all_to_all(picked, 'expert', split_axis=0, concat_axis=1, tiled=True)]
    unnamed x8 -> x7, waiting for transfers between devices: 56.8 us -> 56.1 us
    unnamed x33 -> x35, local copies, waits for them, and re-layouts: 56.8 us -> 56.6 us
  transfers between devices with their start and end apart: 10 -> 9, of which waited for: 8 -> 6; matrix products, arithmetic and copies ran while one was open for 20% -> 22% of each run, Pallas kernels for 0% -> 0%
where the time goes in v1:
time: 627 us; the launch traced here: 618 us
  waiting for transfers between devices  387 us (62%)
  local copies, waits for them, and re-layouts  77.5 us (12%)
  matrix products  48 us (8%)
  blocking collectives  33.5 us (5%)
  other arithmetic  30.7 us (5%)
  starting transfers between devices  26.2 us (4%)
  between operations  14.2 us (2%)
    psum x1, waiting for transfers between devices, body(): lax.psum(jnp.dot(tokens.T, d_logit, preferred_element_type=jnp.float32),...  140 us
    all_gather x1, waiting for transfers between devices, body(): lax.all_gather(w_gate, 'dp', axis=1, tiled=True)  77.5 us
    unnamed x35, local copies, waits for them, and re-layouts  56.6 us
    unnamed x7, waiting for transfers between devices  56.1 us
    all_to_all x1, waiting for transfers between devices, body(): lax.all_to_all(scaled_cot, 'expert', split_axis=0, concat_axis=1, tiled=T...  55 us
    all_to_all x1, waiting for transfers between devices, body(): lax.all_to_all(expert_out, 'expert', split_axis=1, concat_axis=0, tiled=T...  44.8 us
    all_to_all x1, blocking collectives, body(): lax.all_to_all(picked, 'expert', split_axis=0, concat_axis=1, tiled=True)  33.5 us
    unnamed x2, other arithmetic  25.3 us
  transfers between devices with their start and end apart: 9, of which 6 were waited for; matrix products, arithmetic and copies ran while one was open for 22% of the time, Pallas kernels for 0%

profile of v1, /device:TPU:1, one launch (start us, length us, event | category | flops | bytes accessed | tf_op | source)
XLA Modules:
  0.0 617.7 jit_solution(9585926203435499738)
XLA Ops:
  10.8 4.5 gather_fusion.2
  19.4 9.5 %all-to-all-start.3 = ((bf16[16,32,1536]{2,1,0:T(8,128)(2,1)}), bf16[16,32,1536]{2,1,0:T(8,128)(2,1)}, u32[]{:S(2)}, u32[]{:S(2)}) async-start(bf16[16,32,1536]{2,1,0:T(8,128)(2,1)} %multiply_convert_fusion), calls=%async_computation.3 | async-start | bytes 3145728 | tf_op jit(solution)/shard_map/all_to_all | solution.py:80
  31.8 55.0 %all-to-all-done.3 = bf16[16,32,1536]{2,1,0:T(8,128)(2,1)} async-done(((bf16[16,32,1536]{2,1,0:T(8,128)(2,1)}), bf16[16,32,1536]{2,1,0:T(8,128)(2,1)}, u32[]{:S(2)}, u32[]{:S(2)}) %all-to-all-start.3) | async-done | bytes 1572896 | tf_op jit(solution)/shard_map/all_to_all | solution.py:80
  86.8 33.5 %all_to_all.20 = bf16[16,32,1536]{2,1,0:T(8,128)(2,1)} all-to-all(bf16[16,32,1536]{2,1,0:T(8,128)(2,1)} %bitcast.137), channel_id=1, replica_groups=mesh['dp'=8,'expert'=16] {'expert'}, dimensions={0} | all-to-all | bytes 3145728 | tf_op jit(solution)/shard_map/all_to_all | solution.py:69
  126.8 5.6 fusion.5
  132.4 77.5 %all-gather.3.cloned.1.call-done = bf16[1,1536,1024]{2,1,0:T(8,128)(2,1)} async-done(((bf16[1,192,1024]{2,1,0:T(8,128)(2,1)}), bf16[1,1536,1024]{2,1,0:T(8,128)(2,1)}) %all-gather.3.cloned.1.call-update) | async-done | bytes 3145744 | tf_op jit(solution)/shard_map/all_gather | solution.py:65
  209.9 5.5 fusion.9
  215.4 7.5 %multiply_convert_fusion.1 = (bf16[512,1024]{1,0:T(8,128)(2,1)}, bf16[512,1024]{1,0:T(8,128)(2,1)}, bf16[512,1024]{1,0:T(8,128)(2,1)S(1)}) fusion(f32[512,1024]{1,0:T(8,128)} %fusion.9, f32[512,1024]{1,0:T(8,128)} %fusion.5, bf16[512,1536]{1,0:T(8,128)(2,1)} %bitcast.19, bf16[1024,1536]{1,0:T(8,128)(2,1)} %bitcast.10), kind=kOutput, calls=%fused_computation.32 | convolution fusion | flops 1618477056 | bytes 12058624 | tf_op jit(solution)/shard_map/erd,ehd->erh/dot_general | solution.py:82
  223.8 4.9 fusion.1
  228.8 4.6 copy.104
  233.6 8.1 %fusion = bf16[1536,2048]{0,1:T(8,128)(2,1)} fusion(bf16[512,1536]{1,0:T(8,128)(2,1)} %bitcast.142, bf16[1,512,1024]{2,1,0:T(8,128)(2,1)} %bitcast.146, bf16[1,512,1024]{2,1,0:T(8,128)(2,1)} %bitcast.147), kind=kOutput, calls=%fused_computation.4 | convolution fusion | flops 3228565504 | bytes 9961472 | tf_op jit(solution)/shard_map/erc,erk->cek/dot_general | solution.py:23
  241.8 8.7 %copy.102 = bf16[1536,2048]{1,0:T(8,128)(2,1)} copy(bf16[1536,2048]{0,1:T(8,128)(2,1)} %fusion) | data formatting | bytes 12582912
  261.2 12.8 %reduce.2 = bf16[512,1536]{1,0:T(8,128)(2,1)} reduce(bf16[512,1,1536]{2,1,0:T(2,128)(2,1)} %bitcast.133, bf16[]{:T(256)} %broadcast.106), dimensions={1}, to_apply=%bitcast.127.reduce_sub_computation | reduce | bytes 3145730
  274.0 5.0 reshape.254
  278.9 7.2 %all-to-all-start.4 = ((bf16[16,2,24576]{2,1,0:T(2,128)(2,1)}), bf16[16,2,24576]{2,1,0:T(2,128)(2,1)}, u32[]{:S(2)}, u32[]{:S(2)}) async-start(bf16[16,2,24576]{2,1,0:T(2,128)(2,1)} %reshape.254), calls=%async_computation.4 | async-start | bytes 3145728 | tf_op jit(solution)/shard_map/all_to_all | solution.py:92
  294.2 12.6 %reduce.1 = bf16[512,1536]{1,0:T(8,128)(2,1)} reduce(bf16[512,1,1536]{2,1,0:T(2,128)(2,1)} %bitcast.135, bf16[]{:T(256)} %broadcast.106), dimensions={1}, to_apply=%bitcast.128.reduce_sub_computation | reduce | bytes 3145730
  306.8 5.0 reshape.252
  311.7 13.7 %all-to-all-done.4 = bf16[16,2,24576]{2,1,0:T(2,128)(2,1)} async-done(((bf16[16,2,24576]{2,1,0:T(2,128)(2,1)}), bf16[16,2,24576]{2,1,0:T(2,128)(2,1)}, u32[]{:S(2)}, u32[]{:S(2)}) %all-to-all-start.4) | async-done | bytes 1572896 | tf_op jit(solution)/shard_map/all_to_all | solution.py:92
  325.4 4.7 all-to-all-start.2
  330.8 10.0 %reshape.255 = bf16[512,1,1536]{2,1,0:T(2,128)(2,1)} reshape(bf16[16,2,24576]{2,1,0:T(2,128)(2,1)} %all-to-all-done.4) | data formatting | bytes 3145728
  344.2 44.8 %all-to-all-done.2 = bf16[16,2,24576]{2,1,0:T(2,128)(2,1)} async-done(((bf16[16,2,24576]{2,1,0:T(2,128)(2,1)}), bf16[16,2,24576]{2,1,0:T(2,128)(2,1)}, u32[]{:S(2)}, u32[]{:S(2)}) %all-to-all-start.2) | async-done | bytes 1572896 | tf_op jit(solution)/shard_map/all_to_all | solution.py:79
  389.0 10.0 %reshape.253 = bf16[512,1,1536]{2,1,0:T(2,128)(2,1)} reshape(bf16[16,2,24576]{2,1,0:T(2,128)(2,1)} %all-to-all-done.2) | data formatting | bytes 3145728
  410.3 54.7 %reduce-scatter.7.cloned.1.call-done = bf16[192,2048]{1,0:T(8,128)(2,1)} async-done(((bf16[1536,2048]{1,0:T(8,128)(2,1)}), bf16[192,2048]{1,0:T(8,128)(2,1)}) %reduce-scatter.7.cloned.1.call-update) | async-done | bytes 786448
  469.2 140.3 %all-reduce.2.cloned.1.call-done = f32[1536,16]{0,1:T(8,128)} async-done(((f32[1536,16]{0,1:T(8,128)}), f32[1536,16]{0,1:T(8,128)}) %all-reduce.2.cloned.1.call-update) | async-done | bytes 98320 | tf_op jit(solution)/shard_map/psum | solution.py:125
  (84 shorter events, 57.8 us)
Async XLA Ops:
  7.2 2.5 copy-start
  7.2 119.6 %all-gather.5.cloned.1.call-start = ((), (), s32[]{:S(2)}) async-start(), calls=%async_computation.8 | async-start | bytes 3538944 | tf_op jit(solution)/shard_map/all_gather | solution.py:66
  7.9 202.0 %all-gather.3.cloned.1.call-start = ((), (), s32[]{:S(2)}) async-start(), calls=%async_computation.7 | async-start | bytes 3538944 | tf_op jit(solution)/shard_map/all_gather | solution.py:65
  10.8 4.7 copy-start.5
  10.8 5.0 copy-start.1
  19.4 67.4 %all-to-all-start.3 = ((bf16[16,32,1536]{2,1,0:T(8,128)(2,1)}), bf16[16,32,1536]{2,1,0:T(8,128)(2,1)}, u32[]{:S(2)}, u32[]{:S(2)}) async-start(bf16[16,32,1536]{2,1,0:T(8,128)(2,1)} %multiply_convert_fusion), calls=%async_computation.3 | async-start | bytes 3145728 | tf_op jit(solution)/shard_map/all_to_all | solution.py:80
  31.8 88.5 %copy-start.4 = (bf16[1,128,1536]{2,1,0:T(8,128)(2,1)S(1)}, bf16[1,128,1536]{2,1,0:T(8,128)(2,1)}, u32[]{:S(2)}) copy-start(bf16[1,128,1536]{2,1,0:T(8,128)(2,1)} %param.13) | copy-start | bytes 1179652
  122.3 93.1 %all-to-all-start.1 = ((bf16[8,1,128,1536]{3,2,1,0:T(8,128)(2,1)}), bf16[8,1,128,1536]{3,2,1,0:T(8,128)(2,1)}, u32[]{:S(2)}, u32[]{:S(2)}) async-start(bf16[8,1,128,1536]{3,2,1,0:T(8,128)(2,1)} %stack.2), calls=%async_computation.1 | async-start | bytes 6291456 | tf_op jit(solution)/shard_map/all_to_all | solution.py:49
  126.8 281.1 %reduce-scatter.9.cloned.1.call-start = ((), (), s32[]{:S(2)}) async-start(), calls=%async_computation.11 | async-start | bytes 3538944
  222.9 1.0 copy-start.9
  233.4 231.6 %reduce-scatter.7.cloned.1.call-start = ((), (), s32[]{:S(2)}) async-start(), calls=%async_computation.10 | async-start | bytes 7077888
  250.5 4.2 copy-start.7
  250.5 4.2 copy-start.8
  278.9 46.5 %all-to-all-start.4 = ((bf16[16,2,24576]{2,1,0:T(2,128)(2,1)}), bf16[16,2,24576]{2,1,0:T(2,128)(2,1)}, u32[]{:S(2)}, u32[]{:S(2)}) async-start(bf16[16,2,24576]{2,1,0:T(2,128)(2,1)} %reshape.254), calls=%async_computation.4 | async-start | bytes 3145728 | tf_op jit(solution)/shard_map/all_to_all | solution.py:92
  325.4 63.5 %all-to-all-start.2 = ((bf16[16,2,24576]{2,1,0:T(2,128)(2,1)}), bf16[16,2,24576]{2,1,0:T(2,128)(2,1)}, u32[]{:S(2)}, u32[]{:S(2)}) async-start(bf16[16,2,24576]{2,1,0:T(2,128)(2,1)} %reshape.252), calls=%async_computation.2 | async-start | bytes 3145728 | tf_op jit(solution)/shard_map/all_to_all | solution.py:79
  330.1 279.3 %all-reduce.2.cloned.1.call-start = ((), (), s32[]{:S(2)}) async-start(), calls=%async_computation.9 | async-start | bytes 196608 | tf_op jit(solution)/shard_map/psum | solution.py:125
  401.4 1.5 copy-start.3
  401.9 1.4 copy-start.6
  402.9 2.2 copy-start.2
Sparse Core Ops, SparseCore 0:
  9.7 93.4 all-gather.4
  104.8 105.0 all-gather.2
  233.5 79.8 reduce-scatter.8
  315.7 149.2 reduce-scatter.6
  470.2 139.2 all-reduce.1
